TPU v7x, 32 devices: a whole 2x2x4 slice. The times are simulated.
32 devices in a mesh: grp: 2 (over y), ka: 4 (over z), ga: 2 (over x), ba: 2 (over core).
Axes of the slice: x: 2, y: 2, z: 4, core: 2. Of those that a mesh axis runs over, the one named last changes fastest.
Arguments:
- coefficients: bfloat16 [2, 2, 16, 512, 9216], P(None, None, ('grp', 'ka'), 'ba', 'ga'), parts along dimension 2, may hold values from -1 to 1
- occupied: int32 [2, 16], P(None, ('grp', 'ka')), parts along dimension 1, may hold values from 64 to 512
- kweights: float32 [16], P(('grp', 'ka')), parts along dimension 0, may hold values from 0.5 to 2
- owner_map: int32 [1024], P('grp'), parts along dimension 0, may hold values from 0 to 7, as said below
- species: int32 [1024], P('grp'), parts along dimension 0, may hold values from 0 to 1
- positions: float32 [3, 1024], P(None, 'grp'), parts along dimension 1, may hold values from 0 to 100
- multipole: float32 [2, 9, 324], replicated, may hold values from -0.3125 to 0.3125
- widths: float32 [2], replicated, may hold values from 0.05 to 0.3
- potential: float32 [2, 442368], P(None, ('grp', 'ga')), parts along dimension 1, may hold values from -0.013671875 to 0.013671875
Outputs:
- density: float32 [2, 2, 1024, 324], P(None, None, ('grp', 'ka', 'ga', 'ba')), parts along dimension 2
- forces: float32 [3, 1024], P(None, ('grp', 'ka', 'ga', 'ba')), parts along dimension 1
There are 2 independent parts, one for each index of `grp`. A program takes and returns all parts, laid end to end along the dimension named above; an argument that names none is the same for every part. Nothing has to cross between parts.
Inputs may be any that keep to these rules, and one draw needn't show every extreme that they name: `owner_map`: within each aligned block of 256 atoms every owner number is named by exactly 32 atoms.
All inputs are finite; a program needn't handle non-finite values.
Results may differ from a plain program's by a relative error of at most 0.0003.
Values sent between devices are 32-bit elements; how exact they have to be, the bound alone decides.
A program may use at most 192 MiB of HBM per device.

v0:
```python
import jax
import jax.numpy as jnp
from jax import lax
from jax.sharding import PartitionSpec as P

NPROJ = 18
SPECIES = 2
NL = 9
GRID = 96


grid_step = 0.0625
highest = lax.Precision.HIGHEST


def harmonics(start_index, length, widths):
    indices = start_index + jnp.arange(length, dtype=jnp.int32)
    planes = [indices % GRID, indices // GRID % GRID, indices // (GRID * GRID)]
    vectors = []
    for plane_index in planes:
        signed = jnp.where(plane_index >= GRID // 2, plane_index - GRID, plane_index)
        vectors.append(grid_step * signed.astype(jnp.float32))
    along_x, along_y, along_z = vectors
    square = along_x * along_x + along_y * along_y + along_z * along_z
    shapes = jnp.stack(
        [
            jnp.ones_like(square),
            along_x,
            along_y,
            along_z,
            along_x * along_y,
            along_y * along_z,
            along_z * along_x,
            along_x * along_x - along_y * along_y,
            3.0 * along_z * along_z - square,
        ]
    )
    damping = jnp.exp(-widths[:, None] * square[None, :])
    form_table = (damping[:, None, :] * shapes[None, :, :]).reshape(SPECIES * NL, length)
    return (form_table, jnp.stack(vectors, axis=1))


def force_block(moments, places, form_table, vectors, pot_piece):
    smooth = jnp.dot(moments, form_table, precision=highest)
    phases = jnp.dot(places, vectors.T, precision=highest)
    wave_term = pot_piece[0][None, :] * jnp.sin(phases) + pot_piece[1][None, :] * jnp.cos(phases)
    return jnp.dot(smooth * wave_term, vectors, precision=highest)


def local_force(moments, places, pot_piece, start_index, widths):
    length = pot_piece.shape[1]
    pieces = 8
    width_block = length // pieces

    def gblock(running, number):
        offset = number * width_block
        form_table, vectors = harmonics(start_index + offset, width_block, widths)
        segment = lax.dynamic_slice_in_dim(pot_piece, offset, width_block, 1)
        return (running + force_block(moments, places, form_table, vectors, segment), None)

    result, unused = lax.scan(
        gblock, jnp.zeros((moments.shape[0], 3), jnp.float32), jnp.arange(pieces, dtype=jnp.int32)
    )
    return result


def shards(
    coefficients, occupied, kweights, owner_map, species, positions, multipole, widths, potential
):
    spin_count, complex_parts, kcount, bcount, columns = coefficients.shape
    atoms_blk = columns // NPROJ
    kgroups = lax.axis_size("ka")
    bgroups = lax.axis_size("ba")
    owners = kgroups * bgroups
    per_owner = atoms_blk // owners
    owner_index = lax.axis_index(("ka", "ba"))
    group_index = lax.axis_index("ga")
    band_index = lax.axis_index("ba") * bcount + jnp.arange(bcount, dtype=jnp.int32)
    band_mask = (band_index[None, None, :] < occupied[:, :, None]).astype(jnp.bfloat16)
    values = coefficients.reshape(spin_count, complex_parts, kcount, bcount, atoms_blk, NPROJ)
    masked = values * band_mask[:, None, :, :, None, None]
    real_part = jnp.einsum(
        "sckbai,sckbaj->skaij", values, masked, preferred_element_type=jnp.float32
    )
    cross_term = jnp.einsum(
        "skbai,skbaj->skaij", values[:, 0], masked[:, 1], preferred_element_type=jnp.float32
    )
    imag_part = cross_term - jnp.swapaxes(cross_term, 3, 4)
    weighted = jnp.stack([real_part, imag_part], axis=1) * kweights[None, None, :, None, None, None]
    density_local = jnp.sum(weighted, axis=2).reshape(
        spin_count, complex_parts, atoms_blk, NPROJ * NPROJ
    )
    ranking = jnp.argsort(owner_map.reshape(-1, atoms_blk), axis=1, stable=True)
    own_ranks = lax.dynamic_slice_in_dim(ranking, owner_index * per_owner, per_owner, 1)
    summed = lax.psum(density_local, ("ka", "ba"))
    own_rows = lax.dynamic_index_in_dim(own_ranks, group_index, 0, keepdims=False)
    own_density = jnp.take(summed, own_rows, axis=2)
    block_count = own_ranks.shape[0]
    atom_ids = jnp.arange(block_count, dtype=jnp.int32)[:, None] * atoms_blk + own_ranks
    own_atoms = lax.dynamic_index_in_dim(atom_ids, group_index, 0, keepdims=False)
    real_total = jnp.sum(own_density[:, 0], axis=0)
    selector = (
        jnp.take(species, own_atoms)[:, None] == jnp.arange(SPECIES, dtype=jnp.int32)[None, :]
    ).astype(jnp.float32)
    moments = jnp.dot(
        real_total, multipole.reshape(SPECIES * NL, NPROJ * NPROJ).T, precision=highest
    ) * jnp.repeat(selector, NL, axis=1)
    gcount = potential.shape[1]
    all_moments = lax.all_gather(moments, "ga", axis=0, tiled=True)
    places = jnp.take(positions, atom_ids.reshape(-1), axis=1).T
    partial_force = local_force(all_moments, places, potential, group_index * gcount, widths)
    summed_force = lax.psum(partial_force, "ga")
    own_force = lax.dynamic_slice_in_dim(summed_force, group_index * per_owner, per_owner, 0)
    return (own_density, own_force.T)


def solution(mesh):
    placed = (
        P(None, None, ("grp", "ka"), "ba", "ga"),
        P(None, ("grp", "ka")),
        P(("grp", "ka")),
        P("grp"),
        P("grp"),
        P(None, "grp"),
        P(),
        P(),
        P(None, ("grp", "ga")),
    )
    return jax.shard_map(
        shards,
        mesh=mesh,
        in_specs=placed,
        out_specs=(
            P(None, None, ("grp", "ka", "ga", "ba"), None),
            P(None, ("grp", "ka", "ga", "ba")),
        ),
        check_vma=False,
    )
```

profile of v0, /device:TPU:0, one launch (start us, length us, event | category | flops | bytes accessed | tf_op | source)
XLA Modules:
  0.0 663.2 jit_solution(12733213700706561287)
XLA Ops:
  8.1 1.3 reshape.503
  10.0 45.7 %copy.45 = bf16[2,2,2,256,4608]{3,2,4,1,0:T(2,128)(2,1)} copy(bf16[2,2,2,256,4608]{4,3,2,1,0:T(8,128)(2,1)} %param.11) | data formatting | bytes 37748736 | tf_op args[0]
  55.7 45.4 %copy.46 = bf16[2,2,2,256,256,18]{4,3,5,2,1,0:T(8,128)(2,1)} copy(bf16[2,2,2,256,256,18]{3,2,5,4,1,0:T(2,128)(2,1)} %bitcast.68) | data formatting | bytes 37748736 | tf_op jit(solution)/shard_map/reshape | solution.py:80
  101.1 9.1 %slice.35 = bf16[2,1,2,256,256,18]{3,2,5,4,1,0:T(2,128)(2,1)} slice(bf16[2,2,2,256,256,18]{3,2,5,4,1,0:T(2,128)(2,1)} %bitcast.69), slice={[0:2], [0:1], [0:2], [0:256], [0:256], [0:18]} | slice | bytes 18874368 | tf_op jit(solution)/shard_map/slice | solution.py:86
  110.3 16.7 %broadcast_multiply_fusion.2 = bf16[2,2,2,256,256,18]{4,3,5,2,1,0:T(8,128)(2,1)} fusion(bf16[2,2,2,256,256,18]{4,3,5,2,1,0:T(8,128)(2,1)} %copy.46, bf16[2,2,256]{2,1,0:T(2,128)(2,1)S(1)} %compare_convert_fusion), kind=kLoop, calls=%fused_computation.84 | loop fusion | flops 9437184 | bytes 37750784 | tf_op jit(solution)/shard_map/mul | solution.py:81
  127.0 8.4 %slice_bitcast_fusion = bf16[2,2,256,256,18]{3,2,4,1,0:T(8,128)(2,1)} fusion(bf16[2,2,2,256,256,18]{4,3,5,2,1,0:T(8,128)(2,1)} %broadcast_multiply_fusion.2), kind=kLoop, calls=%fused_computation.83 | loop fusion | bytes 18874368 | tf_op jit(solution)/shard_map/squeeze | solution.py:86
  135.4 29.6 %copy.62 = bf16[2,2,2,256,256,18]{3,5,1,2,0,4:T(8,128)(2,1)} copy(bf16[2,2,2,256,256,18]{4,3,5,2,1,0:T(8,128)(2,1)} %broadcast_multiply_fusion.2) | data formatting | bytes 37748736 | tf_op jit(solution)/shard_map/mul | solution.py:81
  165.1 15.5 %copy.50 = bf16[2,2,256,256,18]{2,4,3,1,0:T(8,128)(2,1)} copy(bf16[2,2,256,256,18]{3,2,4,1,0:T(8,128)(2,1)} %slice_bitcast_fusion) | data formatting | bytes 18874368 | tf_op jit(solution)/shard_map/squeeze | solution.py:86
  180.6 13.3 %fusion.40 = f32[2,2,256,18,18]{4,3,2,1,0:T(8,128)} fusion(bf16[2,2,256,256,18]{2,4,3,1,0:T(8,128)(2,1)} %copy.50, bf16[2,1,2,256,256,18]{3,2,5,4,1,0:T(2,128)(2,1)} %slice.35), kind=kOutput, calls=%fused_computation.80 | convolution fusion | flops 169869312 | bytes 20201472 | tf_op jit(solution)/shard_map/skbai,skbaj->skaij/dot_general | solution.py:85
  193.9 14.0 %copy.51 = f32[2,2,256,18,18]{3,4,2,1,0:T(8,128)} copy(f32[2,2,256,18,18]{4,3,2,1,0:T(8,128)} %fusion.40) | data formatting | bytes 2654208 | tf_op jit(solution)/shard_map/skbai,skbaj->skaij/dot_general | solution.py:85
  207.9 14.1 %fusion.41 = f32[2,1,2,256,18,18]{5,4,3,2,0,1:T(8,128)} fusion(f32[2,2,256,18,18]{4,3,2,1,0:T(8,128)} %fusion.40, f32[2,2,256,18,18]{3,4,2,1,0:T(8,128)} %copy.51), kind=kLoop, calls=%fused_computation.82 | loop fusion | flops 331776 | bytes 3981312 | tf_op jit(solution)/shard_map/stack | solution.py:89
  221.9 11.4 %copy.53 = f32[2,1,2,256,18,18]{3,2,5,4,1,0:T(2,128)S(1)} copy(f32[2,1,2,256,18,18]{5,4,3,2,0,1:T(8,128)} %fusion.41) | data formatting | bytes 2654208 | tf_op jit(solution)/shard_map/stack | solution.py:89
  233.4 21.8 %fusion.42 = f32[2,1,2,256,18,18]{4,5,2,0,3,1:T(8,128)} fusion(bf16[2,2,2,256,256,18]{3,5,1,2,0,4:T(8,128)(2,1)} %copy.62, bf16[2,2,2,256,256,18]{3,2,5,4,1,0:T(2,128)(2,1)} %bitcast.70), kind=kOutput, calls=%fused_computation.85 | convolution fusion | flops 339738624 | bytes 39075840 | tf_op jit(solution)/shard_map/sckbai,sckbaj->skaij/dot_general | solution.py:82
  255.1 11.6 %copy.52 = f32[2,1,2,256,18,18]{3,2,5,4,1,0:T(2,128)S(1)} copy(f32[2,1,2,256,18,18]{4,5,2,0,3,1:T(8,128)} %fusion.42) | data formatting | bytes 2654208 | tf_op jit(solution)/shard_map/stack | solution.py:89
  266.8 3.7 fusion.45
  271.6 2.4 copy.56
  278.9 60.1 %all-reduce.2.cloned.1.call-done = f32[2,2,256,324]{3,1,2,0:T(2,128)} async-done(((f32[2,2,256,324]{3,1,2,0:T(2,128)}), f32[2,2,256,324]{3,1,2,0:T(2,128)}) %all-reduce.2.cloned.1.call-update) | async-done | bytes 1327120 | tf_op jit(solution)/shard_map/psum | solution.py:95
  339.0 2.2 gather_fusion
  342.3 4.4 all-gather
  346.8 303.3 %while.14 = (s32[]{:T(128)}, f32[64,3]{0,1:T(4,128)}, f32[2,1]{0,1:T(1,128)S(1)}, s32[8]{0:T(128)S(1)}, s32[]{:T(128)}, /*index=5*/f32[64,18]{0,1:T(8,128)S(1)},...) while((s32[]{:T(128)}, f32[64,3]{0,1:T(4,128)}, ...), condition=%wide.region_5.6_spmd.clone, body=%wide.region_4.5_spmd.clone.sunk | while | flops 262103424 | bytes 21960220 | solution.py:61
  351.1 1.2 add_subtract_fusion.2
  353.7 1.2 mul.712
  356.1 3.7 fusion.77
  359.8 1.3 dynamic-slice_reduce_fusion.3
  361.2 18.2 %convolution_multiply_fusion.3 = f32[13824,64]{0,1:T(8,128)} fusion(f32[18,13824]{1,0:T(8,128)} %mul.712, f32[64,18]{0,1:T(8,128)S(1)} %get-tuple-element.353, f32[13824,64]{0,1:T(8,128)S(1)} %fusion.77, f32[13824]{0:T(1024)S(1)} %get-tuple-element.318, f32[13824]{0:T(1024)S(1)} %get-tuple-element.319), kind=kOutput, calls=%fused_computation.3.clone.1 | convolution fusion | flops 194641920 | bytes 8188416 | tf_op jit(solution)/shard_map/while/body/eval_jaxpr/dot_general | solution.py:44
  379.4 5.5 convolution_add_fusion.2
  389.0 1.2 add_subtract_fusion.2
  394.0 3.7 fusion.77
  397.7 1.3 dynamic-slice_reduce_fusion.3
  399.1 18.2 %convolution_multiply_fusion.3 = f32[13824,64]{0,1:T(8,128)} fusion(f32[18,13824]{1,0:T(8,128)} %mul.712, f32[64,18]{0,1:T(8,128)S(1)} %get-tuple-element.353, f32[13824,64]{0,1:T(8,128)S(1)} %fusion.77, f32[13824]{0:T(1024)S(1)} %get-tuple-element.318, f32[13824]{0:T(1024)S(1)} %get-tuple-element.319), kind=kOutput, calls=%fused_computation.3.clone.1 | convolution fusion | flops 194641920 | bytes 8188416 | tf_op jit(solution)/shard_map/while/body/eval_jaxpr/dot_general | solution.py:44
  417.3 5.5 convolution_add_fusion.2
  426.9 1.2 add_subtract_fusion.2
  431.9 3.7 fusion.77
  435.6 1.3 dynamic-slice_reduce_fusion.3
  436.9 18.2 %convolution_multiply_fusion.3 = f32[13824,64]{0,1:T(8,128)} fusion(f32[18,13824]{1,0:T(8,128)} %mul.712, f32[64,18]{0,1:T(8,128)S(1)} %get-tuple-element.353, f32[13824,64]{0,1:T(8,128)S(1)} %fusion.77, f32[13824]{0:T(1024)S(1)} %get-tuple-element.318, f32[13824]{0:T(1024)S(1)} %get-tuple-element.319), kind=kOutput, calls=%fused_computation.3.clone.1 | convolution fusion | flops 194641920 | bytes 8188416 | tf_op jit(solution)/shard_map/while/body/eval_jaxpr/dot_general | solution.py:44
  455.2 5.5 convolution_add_fusion.2
  464.8 1.2 add_subtract_fusion.2
  467.4 1.2 mul.712
  469.8 3.7 fusion.77
  473.5 1.3 dynamic-slice_reduce_fusion.3
  474.8 18.2 %convolution_multiply_fusion.3 = f32[13824,64]{0,1:T(8,128)} fusion(f32[18,13824]{1,0:T(8,128)} %mul.712, f32[64,18]{0,1:T(8,128)S(1)} %get-tuple-element.353, f32[13824,64]{0,1:T(8,128)S(1)} %fusion.77, f32[13824]{0:T(1024)S(1)} %get-tuple-element.318, f32[13824]{0:T(1024)S(1)} %get-tuple-element.319), kind=kOutput, calls=%fused_computation.3.clone.1 | convolution fusion | flops 194641920 | bytes 8188416 | tf_op jit(solution)/shard_map/while/body/eval_jaxpr/dot_general | solution.py:44
  493.0 5.5 convolution_add_fusion.2
  502.7 1.2 add_subtract_fusion.2
  505.2 1.2 mul.712
  507.7 3.7 fusion.77
  511.4 1.3 dynamic-slice_reduce_fusion.3
  512.7 18.2 %convolution_multiply_fusion.3 = f32[13824,64]{0,1:T(8,128)} fusion(f32[18,13824]{1,0:T(8,128)} %mul.712, f32[64,18]{0,1:T(8,128)S(1)} %get-tuple-element.353, f32[13824,64]{0,1:T(8,128)S(1)} %fusion.77, f32[13824]{0:T(1024)S(1)} %get-tuple-element.318, f32[13824]{0:T(1024)S(1)} %get-tuple-element.319), kind=kOutput, calls=%fused_computation.3.clone.1 | convolution fusion | flops 194641920 | bytes 8188416 | tf_op jit(solution)/shard_map/while/body/eval_jaxpr/dot_general | solution.py:44
  530.9 5.5 convolution_add_fusion.2
  540.6 1.2 add_subtract_fusion.2
  545.6 3.7 fusion.77
  549.3 1.3 dynamic-slice_reduce_fusion.3
  550.6 18.2 %convolution_multiply_fusion.3 = f32[13824,64]{0,1:T(8,128)} fusion(f32[18,13824]{1,0:T(8,128)} %mul.712, f32[64,18]{0,1:T(8,128)S(1)} %get-tuple-element.353, f32[13824,64]{0,1:T(8,128)S(1)} %fusion.77, f32[13824]{0:T(1024)S(1)} %get-tuple-element.318, f32[13824]{0:T(1024)S(1)} %get-tuple-element.319), kind=kOutput, calls=%fused_computation.3.clone.1 | convolution fusion | flops 194641920 | bytes 8188416 | tf_op jit(solution)/shard_map/while/body/eval_jaxpr/dot_general | solution.py:44
  568.8 5.5 convolution_add_fusion.2
  578.5 1.2 add_subtract_fusion.2
  583.5 3.7 fusion.77
  587.2 1.3 dynamic-slice_reduce_fusion.3
  588.5 18.2 %convolution_multiply_fusion.3 = f32[13824,64]{0,1:T(8,128)} fusion(f32[18,13824]{1,0:T(8,128)} %mul.712, f32[64,18]{0,1:T(8,128)S(1)} %get-tuple-element.353, f32[13824,64]{0,1:T(8,128)S(1)} %fusion.77, f32[13824]{0:T(1024)S(1)} %get-tuple-element.318, f32[13824]{0:T(1024)S(1)} %get-tuple-element.319), kind=kOutput, calls=%fused_computation.3.clone.1 | convolution fusion | flops 194641920 | bytes 8188416 | tf_op jit(solution)/shard_map/while/body/eval_jaxpr/dot_general | solution.py:44
  606.7 5.5 convolution_add_fusion.2
  616.3 1.2 add_subtract_fusion.2
  621.4 3.7 fusion.77
  625.1 1.3 dynamic-slice_reduce_fusion.3
  626.4 18.2 %convolution_multiply_fusion.3 = f32[13824,64]{0,1:T(8,128)} fusion(f32[18,13824]{1,0:T(8,128)} %mul.712, f32[64,18]{0,1:T(8,128)S(1)} %get-tuple-element.353, f32[13824,64]{0,1:T(8,128)S(1)} %fusion.77, f32[13824]{0:T(1024)S(1)} %get-tuple-element.318, f32[13824]{0:T(1024)S(1)} %get-tuple-element.319), kind=kOutput, calls=%fused_computation.3.clone.1 | convolution fusion | flops 194641920 | bytes 8188416 | tf_op jit(solution)/shard_map/while/body/eval_jaxpr/dot_general | solution.py:44
  644.6 5.5 convolution_add_fusion.2
  650.2 4.9 psum.15
  (259 shorter events, 62.5 us)
Async XLA Ops:
  8.0 267.3 %copy-start = (s32[512]{0:T(512)S(1)}, s32[512]{0:T(512)}, u32[]{:S(2)}) copy-start(s32[512]{0:T(512)} %param.15) | copy-start | bytes 6148
  8.0 266.3 %sort.19.cloned.1.call-start = ((), (), s32[]{:S(2)}) async-start(), calls=%async_computation.1 | async-start | bytes 12320 | tf_op jit(solution)/shard_map/jit(argsort)/sort | solution.py:93
  9.9 329.0 %all-reduce.2.cloned.1.call-start = ((), (), s32[]{:S(2)}) async-start(), calls=%async_computation | async-start | bytes 3145728 | tf_op jit(solution)/shard_map/psum | solution.py:95
  101.1 9.1 %copy-start.8 = (s32[2,2]{1,0:T(2,128)S(1)}, s32[2,2]{1,0:T(2,128)}, u32[]{:S(2)}) copy-start(s32[2,2]{1,0:T(2,128)} %param.12) | copy-start | bytes 52
  255.1 11.6 %copy-start.9 = (f32[2]{0:T(128)S(1)}, f32[2]{0:T(128)}, u32[]{:S(2)}) copy-start(f32[2]{0:T(128)} %param.13) | copy-start | bytes 28
  270.5 3.6 copy-start.10
  270.5 3.6 copy-start.4
  270.6 3.6 copy-start.7
  347.0 1.2 copy-start.11
  347.0 6.4 copy-start.5
  355.3 0.8 copy-start.1
  356.1 3.7 copy-start.2
  356.1 3.7 copy-start.3
  379.4 5.5 copy-start.6
  379.4 5.5 copy-start.12
  384.9 1.2 copy-start.11
  384.9 6.4 copy-start.5
  393.2 0.8 copy-start.1
  394.0 3.7 copy-start.2
  394.0 3.7 copy-start.3
  417.3 5.5 copy-start.6
  417.3 5.5 copy-start.12
  422.8 1.2 copy-start.11
  422.8 6.4 copy-start.5
  431.0 0.8 copy-start.1
  431.9 3.7 copy-start.2
  431.9 3.7 copy-start.3
  455.2 5.5 copy-start.6
  455.2 5.5 copy-start.12
  460.7 1.2 copy-start.11
  460.7 6.4 copy-start.5
  468.9 0.8 copy-start.1
  469.8 3.7 copy-start.2
  469.8 3.7 copy-start.3
  493.0 5.5 copy-start.6
  493.0 5.5 copy-start.12
  498.6 1.2 copy-start.11
  498.6 6.4 copy-start.5
  506.8 0.8 copy-start.1
  507.7 3.7 copy-start.2
  507.7 3.7 copy-start.3
  530.9 5.5 copy-start.6
  530.9 5.5 copy-start.12
  536.5 1.2 copy-start.11
  536.5 6.4 copy-start.5
  544.7 0.8 copy-start.1
  545.6 3.7 copy-start.2
  545.6 3.7 copy-start.3
  568.8 5.5 copy-start.6
  568.8 5.5 copy-start.12
  574.4 1.2 copy-start.11
  574.4 6.4 copy-start.5
  582.6 0.8 copy-start.1
  583.5 3.7 copy-start.2
  583.5 3.7 copy-start.3
  606.7 5.5 copy-start.6
  606.7 5.5 copy-start.12
  612.3 1.2 copy-start.11
  612.3 6.4 copy-start.5
  620.5 0.8 copy-start.1
  621.3 3.7 copy-start.2
  621.4 3.7 copy-start.3
  644.6 5.5 copy-start.6
  644.6 5.5 copy-start.12
Sparse Core Ops, SparseCore 0:
  11.7 2.2 sort.21.cloned.1.call-done
  (1 shorter events, 0.0 us)
Sparse Core Ops, SparseCore 1:
  274.1 64.8 all-reduce.1
where the time goes:
time: 668 us; the launch traced here: 663 us
  matrix products  255 us (38%)
  local copies, waits for them, and re-layouts  234 us (35%)
  other arithmetic  83.3 us (12%)
  waiting for transfers between devices  60.1 us (9%)
  between operations  15.7 us (2%)
  blocking collectives  9.31 us (1%)
    dot_general x8, matrix products, force_block(): smooth = jnp.dot(moments, form_table, precision=highest)  146 us
    psum x1, waiting for transfers between devices, shards(): summed = lax.psum(density_local, ('ka', 'ba'))  60.1 us
    unnamed x19, local copies, waits for them, and re-layouts  47.3 us
    reshape x1, local copies, waits for them, and re-layouts, shards(): coefficients.reshape(spin_count, complex_parts, kcount, bcount, atoms_blk...  45.4 us
    dot_general x8, matrix products, force_block(): return jnp.dot(smooth * wave_term, vectors, precision=highest)  44.3 us
    mul x1, local copies, waits for them, and re-layouts, shards(): masked = values * band_mask[:, None, :, :, None, None]  29.6 us
    dot_general x8, matrix products, force_block(): phases = jnp.dot(places, vectors.T, precision=highest)  29.6 us
    squeeze x2, local copies, waits for them, and re-layouts, shards(): masked[:, 1]  23.9 us
  transfers between devices with their start and end apart: 1, of which 1 were waited for; matrix products, arithmetic and copies ran while one was open for 1% of the time, Pallas kernels for 0%

commit v1 on v0

v1 whole, which is shorter than its diff:
```python
import functools
import math

import jax
import jax.numpy as jnp
import numpy as np
from jax import lax
from jax.experimental import pallas as pl
from jax.experimental.pallas import tpu as pltpu
from jax.sharding import PartitionSpec as P

NPROJ = 18
SPECIES = 2
NL = 9
GRID = 96
LANES = 128

grid_step = 0.0625
highest = lax.Precision.HIGHEST


def group_width():
    return NPROJ * LANES // math.gcd(NPROJ, LANES)


@functools.lru_cache(None)
def gram_tables():
    tiles = group_width() // LANES
    lane = np.arange(LANES)
    same, pick = [], []
    for t in range(tiles):
        rows = t * LANES + lane
        other = np.where(lane < LANES // 2, (t + 1) * LANES + lane, (t - 1) * LANES + lane)
        cols = np.concatenate([rows, other])
        same.append(rows[:, None] // NPROJ == cols[None, :] // NPROJ)
        pick.append(cols[:, None] % NPROJ == lane[None, :])
    return np.stack(same).astype(np.float32), np.stack(pick).astype(np.float32)


@functools.lru_cache(None)
def monomials():
    powers = [
        (i, j, k) for i in range(4) for j in range(4 - i) for k in range(4 - i - j)
    ]
    shapes = [
        {(0, 0, 0): 1.0},
        {(1, 0, 0): 1.0},
        {(0, 1, 0): 1.0},
        {(0, 0, 1): 1.0},
        {(1, 1, 0): 1.0},
        {(0, 1, 1): 1.0},
        {(1, 0, 1): 1.0},
        {(2, 0, 0): 1.0, (0, 2, 0): -1.0},
        {(0, 0, 2): 2.0, (2, 0, 0): -1.0, (0, 2, 0): -1.0},
    ]
    table = np.zeros((4, 16, 3, NL), np.float32)
    for c in range(3):
        for l, terms in enumerate(shapes):
            for power, value in terms.items():
                i, j, k = (p + (axis == c) for axis, p in enumerate(power))
                table[i, j * 4 + k, c, l] += value
    return table


def gram_kernel(occ_ref, weight_ref, x_ref, same_ref, pick_ref, out_ref, rows_ref):
    spin = pl.program_id(0)
    kcount, bcount, width = x_ref.shape[2:]
    tiles = width // LANES
    atoms = width // NPROJ
    band = lax.broadcasted_iota(jnp.int32, (bcount, LANES), 0)
    masks = [
        (band < occ_ref[spin, k]).astype(jnp.float32).astype(jnp.bfloat16)
        for k in range(kcount)
    ]
    low = lax.broadcasted_iota(jnp.int32, (bcount, LANES), 1) < LANES // 2
    for t in range(tiles):
        here = slice(t * LANES, (t + 1) * LANES)
        before = slice(max(t - 1, 0) * LANES, max(t - 1, 0) * LANES + LANES)
        after = slice(min(t + 1, tiles - 1) * LANES, min(t + 1, tiles - 1) * LANES + LANES)
        real, imag = None, None
        for k in range(kcount):
            windows, turned = [], []
            for c in range(2):
                own = x_ref[0, c, k, :, here]
                other = jnp.where(low, x_ref[0, c, k, :, after], x_ref[0, c, k, :, before])
                windows.append(jnp.concatenate([own * masks[k], other * masks[k]], axis=1))
                turned.append(own.T)

            def dot(a, b):
                return jnp.dot(turned[a], windows[b], preferred_element_type=jnp.float32)

            weight = weight_ref[k]
            re = (dot(0, 0) + dot(1, 1)) * weight
            im = (dot(0, 1) - dot(1, 0)) * weight
            real = re if real is None else real + re
            imag = im if imag is None else imag + im
        pick = pick_ref[t]
        for c, value in enumerate((real, imag)):
            value = value * same_ref[t].astype(jnp.float32)
            high = value.astype(jnp.bfloat16)
            rest = (value - high.astype(jnp.float32)).astype(jnp.bfloat16)
            rows_ref[c, here, :] = jnp.dot(
                high, pick, preferred_element_type=jnp.float32
            ) + jnp.dot(rest, pick, preferred_element_type=jnp.float32)
    lane = lax.broadcasted_iota(jnp.int32, (atoms, LANES), 1)
    for c in range(2):
        sums = [None] * (out_ref.shape[3] // LANES)
        for i in range(NPROJ):
            piece = rows_ref[c, pl.ds(i, atoms, stride=NPROJ), :]
            at, offset = divmod(i * NPROJ, LANES)
            if offset:
                piece = pltpu.roll(piece, offset, 1)
            parts = [(at, piece)]
            if offset + NPROJ > LANES:
                parts = [
                    (at, jnp.where(lane >= offset, piece, 0.0)),
                    (at + 1, jnp.where(lane >= offset, 0.0, piece)),
                ]
            for tile, part in parts:
                sums[tile] = part if sums[tile] is None else sums[tile] + part
        for tile, total in enumerate(sums):
            out_ref[0, c, :, tile * LANES : (tile + 1) * LANES] = total


def gram(coefficients, held, kweights):
    spins, parts, kcount, bcount, columns = coefficients.shape
    width = group_width()
    groups = columns // width
    atoms = width // NPROJ
    padded = -(-NPROJ * NPROJ // LANES) * LANES
    same, pick = gram_tables()
    tiles = width // LANES
    return pl.pallas_call(
        gram_kernel,
        grid=(spins, groups),
        out_shape=jax.ShapeDtypeStruct((spins, parts, columns // NPROJ, padded), jnp.float32),
        in_specs=[
            pl.BlockSpec(memory_space=pltpu.SMEM),
            pl.BlockSpec(memory_space=pltpu.SMEM),
            pl.BlockSpec((1, parts, kcount, bcount, width), lambda s, g: (s, 0, 0, 0, g)),
            pl.BlockSpec((tiles, LANES, 2 * LANES), lambda s, g: (0, 0, 0)),
            pl.BlockSpec((tiles, 2 * LANES, LANES), lambda s, g: (0, 0, 0)),
        ],
        out_specs=pl.BlockSpec((1, parts, atoms, padded), lambda s, g: (s, 0, g, 0)),
        scratch_shapes=[pltpu.VMEM((parts, width, LANES), jnp.float32)],
        compiler_params=pltpu.CompilerParams(
            dimension_semantics=("arbitrary", "arbitrary"), vmem_limit_bytes=40 * 2**20
        ),
        cost_estimate=pl.CostEstimate(
            flops=16 * spins * kcount * bcount * columns * 2 * LANES,
            bytes_accessed=coefficients.size * 2,
            transcendentals=0,
        ),
    )(held, kweights, coefficients, jnp.asarray(same, jnp.bfloat16), jnp.asarray(pick, jnp.bfloat16))


def signed_steps(index):
    return grid_step * jnp.where(index >= GRID // 2, index - GRID, index).astype(jnp.float32)


def wave_sums(places, spread, potential, first_plane):
    atoms = places.shape[1]
    planes = potential.shape[1] // (GRID * GRID)
    line = signed_steps(jnp.arange(GRID, dtype=jnp.int32))
    depth = signed_steps(first_plane + jnp.arange(planes, dtype=jnp.int32))

    def factor(axis, steps):
        angle = places[axis][:, None] * steps[None, :]
        damp = jnp.exp(-spread[:, None] * (steps * steps)[None, :])
        return damp * jnp.cos(angle), damp * jnp.sin(angle)

    cos_x, sin_x = factor(0, line)
    cos_y, sin_y = factor(1, line)
    cos_z, sin_z = factor(2, depth)
    power_x = jnp.stack([jnp.ones_like(line), line, line * line, line * line * line])
    left = jnp.stack(
        [
            jnp.concatenate([cos_x, sin_x], axis=1),
            jnp.concatenate([sin_x, -cos_x], axis=1),
        ]
    )
    left = left[:, None] * jnp.concatenate([power_x, power_x], axis=1)[None, :, None, :]
    grid = potential.reshape(2, planes * GRID, GRID)
    right = jnp.concatenate([grid[1], grid[0]], axis=1)
    along = lax.dot_general(
        left.reshape(8 * atoms, 2 * GRID), right, (((1,), (1,)), ((), ())), precision=highest
    ).reshape(2, 4, atoms, planes, GRID)
    cos_yz = cos_z[:, :, None] * cos_y[:, None, :] - sin_z[:, :, None] * sin_y[:, None, :]
    sin_yz = cos_z[:, :, None] * sin_y[:, None, :] + sin_z[:, :, None] * cos_y[:, None, :]
    wave = along[0] * cos_yz[None] - along[1] * sin_yz[None]
    power_z = jnp.stack([jnp.ones_like(depth), depth, depth * depth, depth * depth * depth])
    weights = power_z[None, :, :, None] * power_x[:, None, None, :]
    sums = jnp.dot(
        wave.reshape(4 * atoms, planes * GRID),
        weights.reshape(16, planes * GRID).T,
        precision=highest,
    ).reshape(4, atoms, 16)
    return jnp.einsum("ian,incl->acl", sums, jnp.asarray(monomials()), precision=highest)


def shards(
    coefficients, occupied, kweights, owner_map, species, positions, multipole, widths, potential
):
    spins, parts, kcount, bcount, columns = coefficients.shape
    atoms_blk = columns // NPROJ
    owners = lax.axis_size("ka") * lax.axis_size("ba")
    per_owner = atoms_blk // owners
    owner_index = lax.axis_index(("ka", "ba"))
    group_index = lax.axis_index("ga")
    held = occupied - lax.axis_index("ba") * bcount
    density_local = gram(coefficients, held, kweights)

    owner_rows = owner_map.reshape(-1, atoms_blk)
    blocks = owner_rows.shape[0]
    number = jnp.arange(atoms_blk, dtype=jnp.int32)
    ahead = (owner_rows[:, None, :] == owner_rows[:, :, None]) & (
        number[None, None, :] < number[None, :, None]
    )
    spot = owner_rows * per_owner + jnp.sum(ahead.astype(jnp.int32), axis=2)
    my_spot = lax.dynamic_index_in_dim(spot, group_index, 0, keepdims=False)
    route = (number[:, None] == my_spot[None, :]).astype(jnp.float32)
    routed = jnp.einsum(
        "opa,scae->oscpe", route.reshape(owners, per_owner, atoms_blk), density_local, precision=highest
    )
    own_density = lax.psum_scatter(routed, ("ka", "ba"), scatter_dimension=0, tiled=True)[0]
    own_density = own_density[..., : NPROJ * NPROJ]

    mine = owner_index * per_owner + jnp.arange(per_owner, dtype=jnp.int32)
    chosen = spot[:, None, :] == mine[None, :, None]
    places = jnp.sum(
        jnp.where(chosen[None], positions.reshape(3, blocks, 1, atoms_blk), 0.0), axis=3
    ).reshape(3, -1)
    kinds = jnp.sum(jnp.where(chosen, species.reshape(blocks, 1, atoms_blk), 0), axis=2)
    spread = jnp.where(kinds.reshape(-1) == 0, widths[0], widths[1])
    first_plane = group_index * (potential.shape[1] // (GRID * GRID))
    terms = wave_sums(places, spread, potential, first_plane)
    terms = lax.psum(terms.reshape(blocks, per_owner, 3 * NL), "ga")
    own_terms = lax.dynamic_index_in_dim(terms, group_index, 0, keepdims=False)
    own_kinds = lax.dynamic_index_in_dim(kinds, group_index, 0, keepdims=False)

    real_total = jnp.sum(own_density[:, 0], axis=0)
    moments = jnp.dot(
        real_total, multipole.reshape(SPECIES * NL, NPROJ * NPROJ).T, precision=highest
    ).reshape(per_owner, SPECIES, NL)
    picked = own_kinds[:, None] == jnp.arange(SPECIES, dtype=jnp.int32)[None, :]
    own_moments = jnp.sum(jnp.where(picked[:, :, None], moments, 0.0), axis=1)
    own_force = jnp.sum(own_terms.reshape(per_owner, 3, NL) * own_moments[:, None, :], axis=2)
    return (own_density, own_force.T)


def solution(mesh):
    placed = (
        P(None, None, ("grp", "ka"), "ba", "ga"),
        P(None, ("grp", "ka")),
        P(("grp", "ka")),
        P("grp"),
        P("grp"),
        P(None, "grp"),
        P(),
        P(),
        P(None, ("grp", "ga")),
    )
    return jax.shard_map(
        shards,
        mesh=mesh,
        in_specs=placed,
        out_specs=(
            P(None, None, ("grp", "ka", "ga", "ba"), None),
            P(None, ("grp", "ka", "ga", "ba")),
        ),
        check_vma=False,
    )
```

time: 668 us -> 117 us (0.18)
  matrix products: 255 us -> 7.9 us
  local copies, waits for them, and re-layouts: 234 us -> 16.7 us
  other arithmetic: 83.3 us -> 5.55 us
  Pallas kernels: 0 us -> 28.7 us
  waiting for transfers between devices: 60.1 us -> 33.5 us
    dot_general x26 -> x4, matrix products: 255 us -> 7.72 us  [the longest x1 3.66 us: wave_sums(): lax.dot_general(left.reshape(8 * atoms, 2 * GRID), right, (((1,), (1,)),...]
    psum x1 -> x0, waiting for transfers between devices: 60.1 us -> none  [shards(): summed = lax.psum(density_local, ('ka', 'ba'))]
    mul x50 -> x10, other arithmetic: 50.6 us -> 0.6 us  [the longest x2 0.43 us: factor(): return (damp * jnp.cos(angle), damp * jnp.sin(angle))]
    reshape x7 -> x3, local copies, waits for them, and re-layouts: 49.3 us -> 0.79 us  [the longest x1 0.7 us: shards(): owner_rows = owner_map.reshape(-1, atoms_blk)]
    unnamed x19 -> x27, local copies, waits for them, and re-layouts: 47.3 us -> 4.73 us
    mul x9 -> x10, local copies, waits for them, and re-layouts: 39.2 us -> 4.49 us  [the longest x4 3.96 us: wave_sums(): wave = along[0] * cos_yz[None] - along[1] * sin_yz[None]]
    unnamed x1 -> x2, waiting for transfers between devices: 0.02 us -> 33.5 us
    another operation x18 -> x2, local copies, waits for them, and re-layouts: 30.1 us -> 0.01 us  [the longest x1 0.01 us: wave_sums(): jnp.stack([jnp.ones_like(depth), depth, depth * depth, depth * depth * de...]
  transfers between devices with their start and end apart: 1 -> 1, of which waited for: 1 -> 1; matrix products, arithmetic and copies ran while one was open for 1% -> 17% of each run, Pallas kernels for 0% -> 0%
where the time goes in v1:
time: 117 us
  waiting for transfers between devices  33.5 us (29%)
  Pallas kernels  28.7 us (25%)
  local copies, waits for them, and re-layouts  16.7 us (14%)
  between operations  14.4 us (12%)
  blocking collectives  9.82 us (8%)
  matrix products  7.9 us (7%)
  other arithmetic  5.55 us (5%)
    unnamed x2, waiting for transfers between devices  33.5 us
    pallas_call x1, Pallas kernels, gram(): pl.pallas_call(gram_kernel, grid=(spins, groups), out_shape=jax.ShapeDtyp...  28.7 us
    psum x1, blocking collectives, shards(): terms = lax.psum(terms.reshape(blocks, per_owner, 3 * NL), 'ga')  9.82 us
    unnamed x27, local copies, waits for them, and re-layouts  4.73 us
    mul x4, local copies, waits for them, and re-layouts, wave_sums(): wave = along[0] * cos_yz[None] - along[1] * sin_yz[None]  3.96 us
    dot_general x1, matrix products, wave_sums(): lax.dot_general(left.reshape(8 * atoms, 2 * GRID), right, (((1,), (1,)),...  3.66 us
    slice x1, local copies, waits for them, and re-layouts, wave_sums(): right = jnp.concatenate([grid[1], grid[0]], axis=1)  2.35 us
  transfers between devices with their start and end apart: 1, of which 1 were waited for; matrix products, arithmetic and copies ran while one was open for 17% of the time, Pallas kernels for 0%

profile of v1, /device:TPU:0, one launch (start us, length us, event | category | flops | bytes accessed | tf_op | source)
XLA Modules:
  0.0 116.6 jit_solution(12215212392778834694)
XLA Ops:
  7.2 0.0 copy-start
  7.2 0.0 all-reduce.3.cloned.1.call-start
  7.3 0.7 reshape.447
  8.0 0.2 convert_reduce_fusion
  8.3 0.7 broadcast_subtract_fusion.occ_ref
  8.9 0.0 copy-start.1
  8.9 0.7 copy-done.1
  9.6 0.0 copy-start.2
  9.6 1.1 copy-done.2
  10.7 0.0 copy-start.3
  10.7 1.1 copy-done.3
  11.7 28.7 %shard_map.131 = f32[2,2,256,384]{3,2,1,0:T(8,128)S(1)} custom-call(s32[2,2]{1,0:T(2,128)S(1)} %broadcast_subtract_fusion.occ_ref, f32[2]{0:T(128)S(1)} %copy-done.1, bf16[2,2,2,256,4608]{4,3,2,1,0:T(8,128)(2,1)} %x_ref.1, bf16[9,128,256]{2,1,0:T(8,128)(2,1)S(1)} %copy-done.2, bf16[9,256,128]{2,1,0:T(8,128)(2,1)S(1)} %copy-done.3), custom_call_target="tpu_custom_call" | custom-call | flops 19327352832 | bytes 18874368 | tf_op jit(solution)/shard_map/pallas_call | solution.py:133
  40.4 2.1 %fusion.2 = f32[8,2,2,32,384]{4,3,0,2,1:T(8,128)} fusion(f32[2,2,256,384]{3,2,1,0:T(8,128)S(1)} %shard_map.131, s32[256]{0:T(256)S(1)} %bitcast.57, s32[8,32]{1,0:T(8,128)S(1)} %multiply_add_fusion.1), kind=kOutput, calls=%fused_computation.2 | convolution fusion | flops 1208025088 | bytes 3147776 | tf_op jit(solution)/shard_map/opa,scae->oscpe/dot_general | solution.py:222
  42.5 0.0 all-reduce.3.cloned.1.call-update
  42.7 0.1 maximum_maximum_fusion
  42.8 0.4 copy-done.10
  43.2 0.1 broadcast_compare_fusion
  43.3 0.2 select_reduce_fusion.1
  43.5 0.0 copy-done.11
  43.5 0.6 fusion.41
  44.1 1.3 %fusion.24 = f32[2,32]{1,0:T(2,128)S(1)} fusion(s32[2,32]{1,0:T(2,128)S(1)} %select_reduce_fusion.1, f32[]{:T(128)} %bitcast.8, f32[]{:T(128)} %bitcast.7), kind=kLoop, calls=%fused_computation.63 | loop fusion | flops 192 | bytes 520 | tf_op jit(solution)/shard_map/neg | solution.py:169
  45.4 0.1 neg.17
  45.5 0.0 copy-done.9
  45.5 0.1 select_reduce_fusion
  45.6 0.1 mul.425
  45.7 0.1 mul.451
  45.8 0.0 copy-done.6
  45.8 2.4 %slice_reduce_fusion.1 = (f32[110592]{0:T(1024)S(1)}, f32[110592]{0:T(1024)S(1)}) fusion(f32[2,110592]{1,0:T(2,128)S(1)} %copy-done.6), kind=kLoop, calls=%fused_computation.18 | loop fusion | bytes 1769472 | tf_op jit(solution)/shard_map/slice | solution.py:184
  48.1 1.0 squeeze.27
  49.1 1.0 squeeze.28
  50.1 0.1 mul.445
  50.2 0.1 fusion.21
  50.3 0.1 copy.18
  50.4 0.1 copy.19
  50.5 0.3 fusion.17
  50.8 1.1 multiply_subtract_fusion
  52.0 0.2 mul.462
  52.1 0.8 mul.463
  52.9 1.2 %mul.467 = f32[4,64,12,96]{3,2,1,0:T(8,128)S(1)} broadcast(f32[64,12,96]{2,1,0:T(8,128)} %get-tuple-element.5), dimensions={1,2,3} | broadcast | bytes 1474560 | tf_op jit(solution)/shard_map/mul | solution.py:190
  54.2 1.8 %mul.468 = f32[256,1152]{1,0:T(8,128)} reshape(f32[4,64,12,96]{3,2,1,0:T(8,128)S(1)} %mul.467) | data formatting | bytes 2359296 | tf_op jit(solution)/shard_map/mul | solution.py:190
  56.0 0.1 maximum_bitcast_fusion
  56.1 0.9 copy-done.5
  57.0 3.7 %fusion.6 = f32[512,1152]{1,0:T(8,128)S(1)} fusion(f32[512,192]{1,0:T(8,128)S(1)} %bitcast.55, f32[1152,96]{1,0:T(8,128)} %squeeze.28, f32[1152,96]{1,0:T(8,128)S(1)} %copy-done.5), kind=kOutput, calls=%fused_computation.6 | convolution fusion | flops 1359175680 | bytes 3637248 | tf_op jit(solution)/shard_map/dot_general | solution.py:185
  60.7 0.0 copy-done.4
  60.7 0.3 fusion.5
  61.0 0.0 copy-start.8
  61.0 0.0 copy-start.12
  61.0 0.1 pad_maximum_fusion.2
  61.1 0.1 broadcast_multiply_fusion.1
  61.2 0.1 reshape.452
  61.3 1.6 %convolution_bitcast_fusion = f32[4,64,16,1]{1,2,0,3:T(8,128)S(1)} fusion(f32[4,64,1152]{2,1,0:T(8,128)S(1)} %bitcast.54, f32[16,1152,1]{1,0,2:T(8,128)S(1)} %reshape.452), kind=kOutput, calls=%fused_computation.10 | convolution fusion | flops 56623104 | bytes 1269760 | tf_op jit(solution)/shard_map/dot_general | solution.py:193
  62.9 0.0 copy-done.8
  62.9 0.3 convolution_bitcast_fusion.1
  63.2 0.1 reshape.448
  63.3 9.8 %psum.7 = f32[2,32,27]{1,0,2:T(2,128)S(1)} all-reduce(f32[2,32,27]{1,0,2:T(2,128)S(1)} %reshape.448), channel_id=1, replica_groups=mesh['grp'=2,'ka'=4,'ga'=2,'ba'=2] {'ga'}, use_global_device_ids=true, to_apply=%region_4.5 | all-reduce | flops 1728 | bytes 13824 | tf_op jit(solution)/shard_map/psum | solution.py:237
  73.2 0.0 copy-done.12
  73.2 0.6 dynamic-slice
  73.8 33.5 %all-reduce.3.cloned.1.call-done = f32[8,2,2,32,384]{4,3,0,2,1:T(8,128)} async-done(((f32[8,2,2,32,384]{4,3,0,2,1:T(8,128)}), f32[8,2,2,32,384]{4,3,0,2,1:T(8,128)}) %all-reduce.3.cloned.1.call-update) | async-done | bytes 1572880
  107.3 1.6 %dynamic-slice_bitcast_fusion = f32[2,2,32,384]{3,2,1,0:T(8,128)S(1)} fusion(f32[8,2,2,32,384]{4,3,0,2,1:T(8,128)} %all-reduce.3.cloned.1.call-done, u32[]{:T(128)} %bitcast.27), kind=kLoop, calls=%fused_computation.23 | loop fusion | bytes 393220 | tf_op jit(solution)/shard_map/squeeze | solution.py:225
  108.9 0.0 copy-start.7
  108.9 0.0 copy-done
  108.9 0.2 fusion.10
  109.1 0.6 multiply_reduce_fusion
  109.7 0.0 copy-done.7
  (30 shorter events, 0.3 us)
Async XLA Ops:
  7.2 101.8 %copy-start = (f32[2,9,324]{2,0,1:T(2,128)S(1)}, f32[2,9,324]{2,0,1:T(2,128)}, u32[]{:S(2)}) copy-start(f32[2,9,324]{2,0,1:T(2,128)} %param.18) | copy-start | bytes 69988
  7.2 100.1 %all-reduce.3.cloned.1.call-start = ((), (), s32[]{:S(2)}) async-start(), calls=%async_computation | async-start | bytes 3145728
  8.9 0.7 copy-start.1
  9.6 1.1 copy-start.2
  10.7 1.1 copy-start.3
  42.5 0.7 copy-start.10
  42.5 1.0 copy-start.11
  42.5 2.9 %copy-start.9 = (f32[3,512]{1,0:T(4,128)S(1)}, f32[3,512]{1,0:T(4,128)}, u32[]{:S(2)}) copy-start(f32[3,512]{1,0:T(4,128)} %param.17) | copy-start | bytes 18436
  42.5 3.2 %copy-start.6 = (f32[2,110592]{1,0:T(2,128)S(1)}, f32[2,110592]{1,0:T(2,128)}, u32[]{:S(2)}) copy-start(f32[2,110592]{1,0:T(2,128)} %param.20) | copy-start | bytes 2654212
  56.0 1.1 copy-start.5
  57.0 3.7 %copy-start.4 = (f32[256,1152]{1,0:T(8,128)S(1)}, f32[256,1152]{1,0:T(8,128)}, u32[]{:S(2)}) copy-start(f32[256,1152]{1,0:T(8,128)} %mul.468) | copy-start | bytes 3538948
  61.0 1.9 %copy-start.8 = (f32[4,16,3,9]{1,3,0,2:T(8,128)S(1)}, f32[4,16,3,9]{1,3,0,2:T(8,128)}, u32[]{:S(2)}) copy-start(f32[4,16,3,9]{1,3,0,2:T(8,128)} %constant.60.clone) | copy-start | bytes 20740
  61.0 12.2 %copy-start.12 = (u32[32]{0:T(128)S(1)}, u32[32]{0:T(128)}, u32[]{:S(2)}) copy-start(u32[32]{0:T(128)} %constant.66) | copy-start | bytes 388
  108.9 0.8 copy-start.7
Sparse Core Ops, SparseCore 0:
  42.7 64.5 all-reduce.2

commit v2 on v1

--- a/solution.py
+++ b/solution.py
@@ -154,6 +154,111 @@
     )(held, kweights, coefficients, jnp.asarray(same, jnp.bfloat16), jnp.asarray(pick, jnp.bfloat16))
 
 
+def gather_kernel(
+    rows_ref, terms_ref, total_ref, sum_ref, first, held, second, third,
+    send1, recv1, send2, recv2, send3, recv3,
+):
+    mesh_id = pl.DeviceIdType.MESH
+    ka, ba, ga = (lax.axis_size(name) for name in ("ka", "ba", "ga"))
+    k, b, g = (lax.axis_index(name) for name in ("ka", "ba", "ga"))
+    barrier = pltpu.get_barrier_semaphore()
+    for name, me, size in (("ka", k, ka), ("ba", b, ba), ("ga", g, ga)):
+        for step in range(1, size):
+            pl.semaphore_signal(
+                barrier, inc=1, device_id={name: lax.rem(me + step, size)}, device_id_type=mesh_id
+            )
+    pl.semaphore_wait(barrier, ka + ba + ga - 3)
+
+    copies1, copies2, copies3 = {}, {}, {}
+    for turn in list(range(1, ka)) + [0]:
+        to = lax.rem(k + turn, ka)
+        for step in range(1, ba):
+            peer = lax.rem(b + step, ba)
+            copy = pltpu.make_async_remote_copy(
+                src_ref=rows_ref.at[to, peer],
+                dst_ref=first.at[step - 1, turn],
+                send_sem=send1.at[step - 1, turn],
+                recv_sem=recv1.at[step - 1, turn],
+                device_id={"ba": peer},
+                device_id_type=mesh_id,
+            )
+            copy.start()
+            copies1[turn, step] = copy
+    for step in range(1, ga):
+        peer = lax.rem(g + step, ga)
+        copy = pltpu.make_async_remote_copy(
+            src_ref=terms_ref.at[peer],
+            dst_ref=third.at[step - 1],
+            send_sem=send3.at[step - 1],
+            recv_sem=recv3.at[step - 1],
+            device_id={"ga": peer},
+            device_id_type=mesh_id,
+        )
+        copy.start()
+        copies3[step] = copy
+    for turn in range(1, ka):
+        to = lax.rem(k + turn, ka)
+        value = rows_ref[to, b]
+        for step in range(1, ba):
+            copies1[turn, step].wait_recv()
+            value = value + first[step - 1, turn]
+        held[turn - 1] = value
+        copy = pltpu.make_async_remote_copy(
+            src_ref=held.at[turn - 1],
+            dst_ref=second.at[turn - 1],
+            send_sem=send2.at[turn - 1],
+            recv_sem=recv2.at[turn - 1],
+            device_id={"ka": to},
+            device_id_type=mesh_id,
+        )
+        copy.start()
+        copies2[turn] = copy
+    value = rows_ref[k, b]
+    for step in range(1, ba):
+        copies1[0, step].wait_recv()
+        value = value + first[step - 1, 0]
+    terms = terms_ref[g]
+    for step in range(1, ga):
+        copies3[step].wait_recv()
+        terms = terms + third[step - 1]
+    sum_ref[...] = terms
+    for turn in range(1, ka):
+        copies2[turn].wait_recv()
+        value = value + second[turn - 1]
+    total_ref[...] = value
+    for copy in [*copies1.values(), *copies2.values(), *copies3.values()]:
+        copy.wait_send()
+
+
+def gather_sums(rows, terms):
+    ka, ba = rows.shape[:2]
+    chunk, piece = rows.shape[2:], terms.shape[1:]
+    ga = lax.axis_size("ga")
+    vmem = pl.BlockSpec(memory_space=pltpu.VMEM)
+    return pl.pallas_call(
+        gather_kernel,
+        out_shape=(
+            jax.ShapeDtypeStruct(chunk, jnp.float32),
+            jax.ShapeDtypeStruct(piece, jnp.float32),
+        ),
+        in_specs=[vmem, vmem],
+        out_specs=(vmem, vmem),
+        scratch_shapes=[
+            pltpu.VMEM((ba - 1, ka, *chunk), jnp.float32),
+            pltpu.VMEM((ka - 1, *chunk), jnp.float32),
+            pltpu.VMEM((ka - 1, *chunk), jnp.float32),
+            pltpu.VMEM((ga - 1, *piece), jnp.float32),
+            pltpu.SemaphoreType.DMA((ba - 1, ka)),
+            pltpu.SemaphoreType.DMA((ba - 1, ka)),
+            pltpu.SemaphoreType.DMA((ka - 1,)),
+            pltpu.SemaphoreType.DMA((ka - 1,)),
+            pltpu.SemaphoreType.DMA((ga - 1,)),
+            pltpu.SemaphoreType.DMA((ga - 1,)),
+        ],
+        compiler_params=pltpu.CompilerParams(collective_id=0, has_side_effects=True),
+    )(rows, terms)
+
+
 def signed_steps(index):
     return grid_step * jnp.where(index >= GRID // 2, index - GRID, index).astype(jnp.float32)
 
@@ -222,9 +327,6 @@
     routed = jnp.einsum(
         "opa,scae->oscpe", route.reshape(owners, per_owner, atoms_blk), density_local, precision=highest
     )
-    own_density = lax.psum_scatter(routed, ("ka", "ba"), scatter_dimension=0, tiled=True)[0]
-    own_density = own_density[..., : NPROJ * NPROJ]
-
     mine = owner_index * per_owner + jnp.arange(per_owner, dtype=jnp.int32)
     chosen = spot[:, None, :] == mine[None, :, None]
     places = jnp.sum(
@@ -234,8 +336,14 @@
     spread = jnp.where(kinds.reshape(-1) == 0, widths[0], widths[1])
     first_plane = group_index * (potential.shape[1] // (GRID * GRID))
     terms = wave_sums(places, spread, potential, first_plane)
-    terms = lax.psum(terms.reshape(blocks, per_owner, 3 * NL), "ga")
-    own_terms = lax.dynamic_index_in_dim(terms, group_index, 0, keepdims=False)
+    terms = terms.reshape(blocks, per_owner, 3 * NL)
+    terms = jnp.pad(terms, ((0, 0), (0, 0), (0, -3 * NL % LANES)))
+    rows = routed.reshape(
+        lax.axis_size("ka"), lax.axis_size("ba"), spins * parts, per_owner, routed.shape[-1]
+    )
+    total, own_terms = gather_sums(rows, terms)
+    own_density = total.reshape(spins, parts, per_owner, -1)[..., : NPROJ * NPROJ]
+    own_terms = own_terms[:, : 3 * NL]
     own_kinds = lax.dynamic_index_in_dim(kinds, group_index, 0, keepdims=False)
 
     real_total = jnp.sum(own_density[:, 0], axis=0)

time: 117 us -> 94.6 us (0.81)
  the two profiles are of different devices: /device:TPU:0 before, /device:TPU:15 now
where the time goes in v2:
time: 94.6 us; the launch traced here: 94 us
  Pallas kernels  53.6 us (57%)
  local copies, waits for them, and re-layouts  22.2 us (23%)
  other arithmetic  9.16 us (10%)
  matrix products  8.02 us (8%)
  between operations  0.96 us (1%)
    pallas_call x1, Pallas kernels, gram(): pl.pallas_call(gram_kernel, grid=(spins, groups), out_shape=jax.ShapeDtyp...  28.7 us
    pallas_call x1, Pallas kernels, gather_sums(): pl.pallas_call(gather_kernel, out_shape=(jax.ShapeDtypeStruct(chunk, jnp....  24.8 us
    mul x4, local copies, waits for them, and re-layouts, wave_sums(): wave = along[0] * cos_yz[None] - along[1] * sin_yz[None]  8.76 us
    dot_general x1, matrix products, wave_sums(): lax.dot_general(left.reshape(8 * atoms, 2 * GRID), right, (((1,), (1,)),...  3.56 us
    sub x1, other arithmetic, wave_sums(): wave = along[0] * cos_yz[None] - along[1] * sin_yz[None]  3.08 us
    dot_general x1, matrix products, wave_sums(): jnp.dot(wave.reshape(4 * atoms, planes * GRID), weights.reshape(16, plane...  2.99 us
    slice x1, local copies, waits for them, and re-layouts, wave_sums(): right = jnp.concatenate([grid[1], grid[0]], axis=1)  2.35 us

profile of v2, /device:TPU:15, one launch (start us, length us, event | category | flops | bytes accessed | tf_op | source)
XLA Modules:
  0.0 94.0 jit_solution(7042963950691802397)
XLA Ops:
  0.6 0.0 copy-start
  0.6 0.0 copy-start.4
  0.7 0.8 reshape.448
  1.5 0.2 convert_reduce_fusion
  1.7 0.7 broadcast_in_dim.52
  2.4 0.2 select_reduce_fusion.1
  2.6 1.3 %fusion.40 = (f32[1]{0:T(128)}, f32[1]{0:T(128)}) fusion(f32[2]{0:T(128)} %param.19), kind=kLoop, calls=%fused_computation.83 | loop fusion | bytes 16 | tf_op jit(solution)/shard_map/slice | solution.py:336
  3.9 1.3 %fusion.24 = f32[2,32]{1,0:T(2,128)S(1)} fusion(s32[2,32]{1,0:T(2,128)S(1)} %select_reduce_fusion.1, f32[]{:T(128)} %bitcast.8, f32[]{:T(128)} %bitcast.7), kind=kLoop, calls=%fused_computation.61 | loop fusion | flops 192 | bytes 520 | tf_op jit(solution)/shard_map/neg | solution.py:274
  5.2 0.1 neg.17
  5.3 0.1 broadcast_compare_fusion
  5.4 0.7 broadcast_in_dim.58
  6.1 0.1 select_reduce_fusion
  6.2 0.6 fusion.39
  6.8 0.1 mul.421
  6.9 0.1 mul.447
  7.0 0.9 fusion.17
  7.9 0.1 maximum_bitcast_fusion
  8.0 0.0 copy-start.6
  8.1 0.0 copy-start.8
  8.1 0.1 maximum_maximum_fusion
  8.2 0.0 copy-done.4
  8.2 2.4 %slice_reduce_fusion.1 = (f32[110592]{0:T(1024)S(1)}, f32[110592]{0:T(1024)S(1)}) fusion(f32[2,110592]{1,0:T(2,128)S(1)} %copy-done.4), kind=kLoop, calls=%fused_computation.18 | loop fusion | bytes 1769472 | tf_op jit(solution)/shard_map/slice | solution.py:289
  10.6 0.0 copy-done.6
  10.6 0.0 copy-done.8
  10.6 0.2 squeeze.21
  10.8 1.0 %squeeze.22 = f32[1152,96]{1,0:T(8,128)} reshape(f32[110592]{0:T(1024)S(1)} %get-tuple-element.7) | data formatting | bytes 884736 | tf_op jit(solution)/shard_map/squeeze | solution.py:289
  11.8 3.6 %fusion.6 = f32[512,1152]{1,0:T(8,128)S(1)} fusion(f32[512,192]{1,0:T(8,128)S(1)} %bitcast.50, f32[1152,96]{1,0:T(8,128)} %squeeze.22, f32[1152,96]{1,0:T(8,128)S(1)} %squeeze.21), kind=kOutput, calls=%fused_computation.6 | convolution fusion | flops 1359175680 | bytes 3637248 | tf_op jit(solution)/shard_map/dot_general | solution.py:290
  15.4 0.8 mul.441
  16.1 0.1 fusion.21
  16.3 0.1 copy.26
  16.4 0.1 copy.27
  16.4 1.1 %multiply_subtract_fusion = (f32[64,12,96]{2,1,0:T(8,128)S(1)}, f32[64,12,96]{2,1,0:T(8,128)S(1)}) fusion(f32[64,96]{1,0:T(8,128)S(1)} %get-tuple-element.22, f32[64,12]{1,0:T(8,128)S(1)} %copy.27, f32[64,96]{1,0:T(8,128)} %get-tuple-element.23, f32[64,12]{1,0:T(8,128)S(1)} %copy.26), kind=kLoop, calls=%fused_computation.15 | loop fusion | flops 442368 | bytes 645120 | tf_op jit(solution)/shard_map/sub | solution.py:293
  17.6 1.5 %mul.458 = f32[4,64,12,96]{3,2,1,0:T(8,128)} broadcast(f32[64,12,96]{2,1,0:T(8,128)S(1)} %get-tuple-element.8), dimensions={1,2,3} | broadcast | bytes 1474560 | tf_op jit(solution)/shard_map/mul | solution.py:295
  19.1 2.9 %mul.459 = f32[256,1152]{1,0:T(8,128)} reshape(f32[4,64,12,96]{3,2,1,0:T(8,128)} %mul.458) | data formatting | bytes 2359296 | tf_op jit(solution)/shard_map/mul | solution.py:295
  22.0 1.5 %mul.463 = f32[4,64,12,96]{3,2,1,0:T(8,128)} broadcast(f32[64,12,96]{2,1,0:T(8,128)S(1)} %get-tuple-element.9), dimensions={1,2,3} | broadcast | bytes 1474560 | tf_op jit(solution)/shard_map/mul | solution.py:295
  23.5 2.9 %mul.464 = f32[256,1152]{1,0:T(8,128)} reshape(f32[4,64,12,96]{3,2,1,0:T(8,128)} %mul.463) | data formatting | bytes 2359296 | tf_op jit(solution)/shard_map/mul | solution.py:295
  26.3 0.0 copy-start.7
  26.3 3.1 %fusion.5 = f32[256,1152]{1,0:T(8,128)} fusion(f32[256,1152]{1,0:T(8,128)} %mul.464, f32[512,1152]{1,0:T(8,128)S(1)} %fusion.6, f32[256,1152]{1,0:T(8,128)} %mul.459), kind=kLoop, calls=%fused_computation.4 | loop fusion | flops 884736 | bytes 5898240 | tf_op jit(solution)/shard_map/sub | solution.py:295
  29.4 0.0 copy-start.3
  29.5 0.1 pad_maximum_fusion.2
  29.5 0.0 copy-done.7
  29.6 0.0 copy-done.9
  29.6 0.1 broadcast_multiply_fusion.1
  29.6 0.1 reshape.455
  29.7 3.0 %convolution_bitcast_fusion = f32[4,64,16,1]{1,2,0,3:T(8,128)S(1)} fusion(f32[4,64,1152]{2,1,0:T(8,128)} %bitcast.49, f32[16,1152,1]{1,0,2:T(8,128)S(1)} %reshape.455), kind=kOutput, calls=%fused_computation.10 | convolution fusion | flops 56623104 | bytes 1269760 | tf_op jit(solution)/shard_map/dot_general | solution.py:298
  32.7 0.0 copy-done.5
  32.8 0.3 convolution_bitcast_fusion.1
  33.1 0.1 reshape.450
  33.2 0.1 copy.28
  33.2 0.6 pad.4.terms_ref
  33.9 0.0 copy-done.10
  33.9 0.0 copy-done.1
  33.9 0.0 copy-done.2
  33.9 0.0 copy-done.3
  33.9 28.7 %shard_map.131 = f32[2,2,256,384]{3,2,1,0:T(8,128)S(1)} custom-call(s32[2,2]{1,0:T(2,128)S(1)} %broadcast_subtract_fusion.occ_ref, f32[2]{0:T(128)S(1)} %copy-done.1, bf16[2,2,2,256,4608]{4,3,2,1,0:T(8,128)(2,1)} %x_ref.1, bf16[9,128,256]{2,1,0:T(8,128)(2,1)S(1)} %copy-done.2, bf16[9,256,128]{2,1,0:T(8,128)(2,1)S(1)} %copy-done.3), custom_call_target="tpu_custom_call" | custom-call | flops 19327352832 | bytes 18874368 | tf_op jit(solution)/shard_map/pallas_call | solution.py:133
  62.6 1.0 %fusion.2 = f32[8,2,2,32,384]{4,3,0,2,1:T(8,128)S(1)} fusion(f32[2,2,256,384]{3,2,1,0:T(8,128)S(1)} %shard_map.131, s32[256]{0:T(256)S(1)} %bitcast.54, s32[8,32]{1,0:T(8,128)S(1)} %multiply_add_fusion.1), kind=kOutput, calls=%fused_computation.2 | convolution fusion | flops 1208025088 | bytes 3147776 | tf_op jit(solution)/shard_map/opa,scae->oscpe/dot_general | solution.py:327
  63.6 1.3 %copy.25 = f32[8,2,2,32,384]{4,3,2,1,0:T(8,128)} copy(f32[8,2,2,32,384]{4,3,0,2,1:T(8,128)S(1)} %fusion.2) | data formatting | bytes 3145728 | tf_op jit(solution)/shard_map/opa,scae->oscpe/transpose | solution.py:327
  64.9 24.8 %shard_map.132 = (f32[4,32,384]{2,1,0:T(8,128)}, f32[32,128]{1,0:T(8,128)}) custom-call(f32[4,2,4,32,384]{4,3,2,1,0:T(8,128)} %bitcast.48, f32[2,32,128]{2,1,0:T(8,128)} %pad.4.terms_ref), custom_call_target="tpu_custom_call" | custom-call | tf_op jit(solution)/shard_map/pallas_call | solution.py:238
  89.8 0.9 slice_reduce_fusion.2
  90.7 0.0 copy-done
  90.7 0.2 fusion.10
  90.9 0.8 copy.29
  91.7 0.6 multiply_reduce_fusion
  92.3 1.6 %copy.37 = f32[2,2,32,324]{3,2,1,0:T(8,128)} copy(f32[2,2,32,324]{3,2,1,0:T(8,128)} %bitcast.52) | data formatting | bytes 331776
  (25 shorter events, 0.2 us)
Async XLA Ops:
  0.6 90.1 %copy-start = (f32[2,9,324]{2,0,1:T(2,128)S(1)}, f32[2,9,324]{2,0,1:T(2,128)}, u32[]{:S(2)}) copy-start(f32[2,9,324]{2,0,1:T(2,128)} %param.18) | copy-start | bytes 69988
  0.6 7.6 %copy-start.4 = (f32[2,110592]{1,0:T(2,128)S(1)}, f32[2,110592]{1,0:T(2,128)}, u32[]{:S(2)}) copy-start(f32[2,110592]{1,0:T(2,128)} %param.20) | copy-start | bytes 2654212
  8.0 2.5 %copy-start.6 = (f32[1,96]{1,0:T(1,128)}, f32[1,96]{1,0:T(1,128)S(1)}, u32[]{:S(2)}) copy-start(f32[1,96]{1,0:T(1,128)S(1)} %fusion.34) | copy-start | bytes 1156
  8.1 2.5 %copy-start.8 = (f32[1,96]{1,0:T(1,128)}, f32[1,96]{1,0:T(1,128)S(1)}, u32[]{:S(2)}) copy-start(f32[1,96]{1,0:T(1,128)S(1)} %stack_broadcast_in_dim.3) | copy-start | bytes 1156
  26.3 3.2 %copy-start.7 = (f32[1,96]{1,0:T(1,128)S(1)}, f32[1,96]{1,0:T(1,128)}, u32[]{:S(2)}) copy-start(f32[1,96]{1,0:T(1,128)} %copy-done.6) | copy-start | bytes 1156
  26.3 3.2 %copy-start.9 = (f32[1,96]{1,0:T(1,128)S(1)}, f32[1,96]{1,0:T(1,128)}, u32[]{:S(2)}) copy-start(f32[1,96]{1,0:T(1,128)} %copy-done.8) | copy-start | bytes 1156
  29.4 3.3 %copy-start.5 = (f32[4,16,3,9]{1,3,0,2:T(8,128)S(1)}, f32[4,16,3,9]{1,3,0,2:T(8,128)}, u32[]{:S(2)}) copy-start(f32[4,16,3,9]{1,3,0,2:T(8,128)} %constant.57.clone) | copy-start | bytes 20740
  29.4 4.5 %copy-start.10 = (s32[2,2]{1,0:T(2,128)S(1)}, s32[2,2]{1,0:T(2,128)}, u32[]{:S(2)}) copy-start(s32[2,2]{1,0:T(2,128)} %param.13) | copy-start | bytes 52
  29.4 4.5 %copy-start.1 = (f32[2]{0:T(128)S(1)}, f32[2]{0:T(128)}, u32[]{:S(2)}) copy-start(f32[2]{0:T(128)} %weight_ref.1) | copy-start | bytes 28
  29.4 4.5 %copy-start.2 = (bf16[9,128,256]{2,1,0:T(8,128)(2,1)S(1)}, bf16[9,128,256]{2,1,0:T(8,128)(2,1)}, u32[]{:S(2)}) copy-start(bf16[9,128,256]{2,1,0:T(8,128)(2,1)} %constant.55.clone.same_ref) | copy-start | bytes 1769476
  29.4 4.5 %copy-start.3 = (bf16[9,256,128]{2,1,0:T(8,128)(2,1)S(1)}, bf16[9,256,128]{2,1,0:T(8,128)(2,1)}, u32[]{:S(2)}) copy-start(bf16[9,256,128]{2,1,0:T(8,128)(2,1)} %constant.56.clone.pick_ref) | copy-start | bytes 1769476
